TPU v7x, 256 devices: a whole 4x4x8 slice. The times are simulated.
256 devices in a mesh: samples: 64 (over z, y, x_lo), vblocks: 4 (over x_hi, core).
Axes of the slice: x: 4 (x_hi: 2, x_lo: 2; x = x_hi * 2 + x_lo), y: 4, z: 8, core: 2. Of those that a mesh axis runs over, the one named last changes fastest.
Arguments:
- genotypes: int32 [65536, 4096], P('samples', 'vblocks'), may hold values from 0 to 2
- typed_mask: int32 [4096], P('vblocks'), may hold values 0 or 1
- z_scores: float32 [1024, 4096], P('samples', 'vblocks'), may hold values from -60 to 60
Outputs:
- solution: float32 [1024, 4096], P('samples', 'vblocks')
- imputed: float32 [1024, 4096], P('samples', 'vblocks')
All inputs are finite; a program needn't handle non-finite values. No bound on the sum of `typed_mask` on one device may be relied on, other than what follows from the above.
Results may differ from a plain program's by a relative error of at most 0.0068.
Values may be sent and summed in bfloat16 or wider, within the bound.
No kernel may reach another device: no remote copies, remote signals or barrier semaphores. Data moves between devices by JAX's collectives and lax.ppermute only.
A program may use at most 64 MiB of HBM per device.

v0:
```python
import jax
import jax.numpy as jnp
from jax import lax
from jax.sharding import Mesh, PartitionSpec as P

ITERS = 3
RIDGE = 0.1
EPSILON = 1e-05
BF16 = jnp.bfloat16
F32 = jnp.float32

SAMPLE_AXES = ("z", "y", "xl")
BLOCK_AXES = ("xh", "core")
PLANE_AXES = ("y", "xl")
SIZES = (8, 4, 2, 2, 2)
N_BLOCKS = 4


def shift(block, axis, distance):
    size = lax.axis_size(axis)
    return lax.ppermute(block, axis, [(i, (i + distance) % size) for i in range(size)])


def from_next(block):
    return lax.ppermute(block, BLOCK_AXES, [(i + 1, i) for i in range(N_BLOCKS - 1)])


def from_previous(block):
    return lax.ppermute(block, BLOCK_AXES, [(i, i + 1) for i in range(N_BLOCKS - 1)])


def contract_rows(first_mat, second_mat):
    return lax.dot_general(
        first_mat, second_mat, (((0,), (0,)), ((), ())), preferred_element_type=F32
    )


def rounded(values):
    return lax.reduce_precision(values, exponent_bits=8, mantissa_bits=7)


def split3(vector):
    high = rounded(vector)
    rest = vector - high
    mid = rounded(rest)
    return jnp.concatenate([high, mid, rest - mid], axis=0).astype(BF16)


def times(stacked, matrix, side):
    out = lax.dot_general(
        stacked, matrix, (((1,), (side,)), ((), ())), preferred_element_type=F32
    )
    rows = stacked.shape[0] // 3
    return out[2 * rows :] + out[rows : 2 * rows] + out[:rows]


def add(first, second):
    return (first.astype(F32) + second.astype(F32)).astype(BF16)


def ring_reduce(parts, axis):
    size = lax.axis_size(axis)
    half = size // 2
    here = lax.axis_index(axis).astype(jnp.uint32)

    def part(offset):
        return lax.dynamic_index_in_dim(parts, (here + (offset + size)) & (size - 1), 1, keepdims=False)

    far = part(half)
    right, left = shift(far[:1], axis, 1), shift(far[1:], axis, -1)
    for offset in range(half - 1, 0, -1):
        ahead, behind = part(offset), part(-offset)
        if offset == half - 1:
            ahead = jnp.concatenate([add(ahead[:1], right), ahead[1:]], axis=0)
            behind = jnp.concatenate([behind[:1], add(behind[1:], left)], axis=0)
        else:
            ahead, behind = add(ahead, right), add(behind, left)
        right, left = shift(ahead, axis, 1), shift(behind, axis, -1)
    mine = part(0).astype(F32)
    if half == 1:
        return mine + jnp.concatenate([right, left], axis=0).astype(F32)
    return mine + right.astype(F32) + left.astype(F32)


def exchange(parts, axes):
    return lax.all_to_all(parts, axes, 0, 0, tiled=True)


def to_all(block, axes):
    copies = jnp.broadcast_to(block[None], (lax.axis_size(axes),) + block.shape)
    return exchange(lax.optimization_barrier(copies), axes)


def reduce_over(rows, axes):
    size = lax.axis_size(axes)
    parts = exchange(rows.reshape((size, -1) + rows.shape[1:]), axes)
    return jnp.sum(parts.astype(F32), axis=0)


def line_of(all_sums, all_squares, total_samples):
    coded_sum = jnp.sum(all_sums, axis=0, keepdims=True)
    mean_dosage = (coded_sum + total_samples) / total_samples
    squares = all_squares + 2.0 * coded_sum + total_samples
    variance = squares / total_samples - mean_dosage * mean_dosage
    scale = lax.rsqrt(variance + EPSILON)
    twos = 0.5 * (all_squares + coded_sum)
    zeros = 0.5 * (all_squares - coded_sum)
    ones = total_samples - all_squares
    level = rise = spread = 0.0
    for dosage, count in ((0.0, zeros), (1.0, ones), (2.0, twos)):
        away = dosage - mean_dosage
        value = rounded(away * scale)
        level = level + count * value
        rise = rise + count * value * away
        spread = spread + count * away * away
    slope = jnp.where(spread > 0.0, rise / jnp.where(spread > 0.0, spread, 1.0), scale)
    return level / total_samples, slope


def on_device(genotypes, typed_mask, z_scores):
    samples_dev, width = genotypes.shape
    total_samples = samples_dev * lax.axis_size(SAMPLE_AXES)
    coded = lax.optimization_barrier((genotypes - 1).astype(BF16))
    following = from_next(coded)

    def column_sums(values):
        return jnp.sum(values.astype(F32), axis=0, keepdims=True)

    def centred(row_sums, others, other_sums):
        counts = contract_rows(coded, others)
        return (counts - row_sums[0][:, None] * (other_sums / samples_dev)).astype(BF16)

    sums = column_sums(coded)
    squares = column_sums(coded * coded)
    following_sums = from_next(sums)
    own_part = centred(sums, coded, sums)
    own_sum = lax.psum_scatter(own_part, "z", scatter_dimension=0, tiled=True)

    everyone = to_all(jnp.concatenate([sums, squares], axis=0), ("z", "y"))
    table = jnp.concatenate(
        [everyone[:, 0], jnp.sum(everyone[:, 1], axis=0, keepdims=True)], axis=0
    )
    table, following = lax.optimization_barrier((table, following))
    partner = shift(table, "xl", 1)
    statistics = jnp.concatenate([table[:-1], partner[:-1], table[-1:] + partner[-1:]], axis=0)
    next_statistics = from_next(statistics)

    edge_part = centred(sums, following, following_sums)
    n_place, n_row = lax.axis_size("z"), lax.axis_size("y")
    edge_part = edge_part.reshape(n_row, 2, -1, width).swapaxes(0, 1)
    edge_sum = ring_reduce(edge_part, "y").astype(BF16)
    edge_sum, own_sum = lax.optimization_barrier((edge_sum, own_sum))
    edge_sum = edge_sum.reshape(2, n_place, -1, width).swapaxes(0, 1).reshape(-1, width)
    edge_sum = lax.psum_scatter(edge_sum, "z", scatter_dimension=0, tiled=True)
    edge_sum = edge_sum.reshape(2, -1, width)
    side = lax.axis_index("xl").astype(jnp.uint32)
    kept = lax.dynamic_index_in_dim(edge_sum, side, 0, keepdims=False)
    sent = lax.dynamic_index_in_dim(edge_sum, 1 - side, 0, keepdims=False)
    edge_sum = kept.astype(F32) + shift(sent, "xl", 1).astype(F32)
    own_sum = reduce_over(own_sum, PLANE_AXES)

    def lines(table):
        level, slope = line_of(table[:-1], table[-1:], total_samples)
        off = (table[:-1] - jnp.mean(table[:-1], axis=0, keepdims=True)) * slope
        return level, slope, off

    row_lines = lines(statistics)
    rows = own_sum.shape[0]
    place, plane = lax.axis_index("z"), lax.axis_index(PLANE_AXES)
    n_plane = lax.axis_size(PLANE_AXES)

    def link_rows(within, first_row, column_lines):
        level, slope, off = column_lines
        level_rows, slope_rows, off_rows = [
            lax.dynamic_slice_in_dim(values, first_row, rows, axis=1) for values in row_lines
        ]
        between = lax.dot_general(
            off_rows,
            off,
            (((0,), (0,)), ((), ())),
            precision=lax.Precision.HIGHEST,
            preferred_element_type=F32,
        )
        link = within * slope * slope_rows[0][:, None] + between / samples_dev
        return (link / total_samples + level_rows[0][:, None] * level).astype(BF16)

    own_rows = link_rows(own_sum, (place * n_plane + plane) * rows, row_lines)
    edge_rows = link_rows(edge_sum, (plane * n_place + place) * rows, lines(next_statistics))
    own = to_all(own_rows, PLANE_AXES).reshape(-1, width)
    own = lax.all_gather(own, "z", axis=0, tiled=True)
    edge = to_all(edge_rows, "z").reshape(-1, width)
    edge = to_all(edge, PLANE_AXES).reshape(-1, width)

    def apply_link(vector):
        ahead = from_next(vector)
        mine = split3(vector)
        lower = from_previous(times(mine, edge, 0))
        result = times(mine, own, 1) + 0.5 * times(split3(ahead), edge, 1)
        return result + 0.5 * lower

    def dots(*pairs):
        local = jnp.stack([jnp.sum(a * b, axis=1) for a, b in pairs])
        opposite = [(i, N_BLOCKS - 1 - i) for i in range(N_BLOCKS)]
        near, far = shift(local, "core", 1), shift(local, "xh", 1)
        across = lax.ppermute(local, BLOCK_AXES, opposite)
        return ((local + near) + (far + across))[:, :, None]

    mask = typed_mask[None, :]
    mask_row = mask.astype(F32)
    scores = z_scores

    residual = mask_row * scores
    residual_link = apply_link(residual)
    image = mask_row * residual_link + RIDGE * residual
    norm_now, curvature = dots((residual, residual), (residual, image))
    image_link = apply_link(image)
    direction, direction_link = residual, residual_link
    push, push_link = image, image_link
    step_size = norm_now / curvature
    solution = step_size * direction
    projected = step_size * direction_link
    for iteration in range(1, ITERS):
        residual = residual - step_size * push
        residual_link = residual_link - step_size * push_link
        image = mask_row * residual_link + RIDGE * residual
        norm_next, fresh, cross_a, cross_b, old, lean, size = dots(
            (residual, residual),
            (residual, image),
            (residual, push),
            (direction, image),
            (direction, push),
            (residual, direction),
            (direction, direction),
        )
        ratio = norm_next / norm_now
        curvature = fresh + ratio * (cross_a + cross_b) + ratio * ratio * old
        length = norm_next + ratio * (2.0 * lean) + ratio * ratio * size
        step_size = norm_next / jnp.maximum(curvature, 0.1 * RIDGE * length)
        if iteration + 1 < ITERS:
            image_link = apply_link(image)
            push_link = image_link + ratio * push_link
            push = image + ratio * push
        direction = residual + ratio * direction
        direction_link = residual_link + ratio * direction_link
        solution = solution + step_size * direction
        projected = projected + step_size * direction_link
        norm_now = norm_next
    imputed = jnp.where(mask == 1, scores, projected)

    return (solution, imputed)


def solution(mesh):
    fine = Mesh(mesh.devices.reshape(SIZES), SAMPLE_AXES + BLOCK_AXES)
    placed = (P(SAMPLE_AXES, BLOCK_AXES), P(BLOCK_AXES), P(SAMPLE_AXES, BLOCK_AXES))

    return jax.shard_map(
        on_device,
        mesh=fine,
        in_specs=placed,
        out_specs=(P(SAMPLE_AXES, BLOCK_AXES), P(SAMPLE_AXES, BLOCK_AXES)),
        check_vma=False,
    )
```

profile of v0, /device:TPU:1, one launch (start us, length us, event | category | flops | bytes accessed | tf_op | source)
XLA Modules:
  0.0 207.2 jit_solution(15193025604750960324)
XLA Ops:
  10.0 5.1 %collective-permute-start = (bf16[1024,1024]{1,0:T(8,128)(2,1)S(1)}, bf16[1024,1024]{1,0:T(8,128)(2,1)}, u32[]{:S(2)}, u32[]{:S(2)}) collective-permute-start(bf16[1024,1024]{1,0:T(8,128)(2,1)S(1)} %add_convert_fusion), channel_id=1, source_target_pairs={{1,0},{2,1},{3,2},{5,4},{6,5},{7,6},{9,8},{10,9},{11,10},{13,12},{... | collective-permute-start | bytes 6291464 | tf_op jit(solution)/shard_map/ppermute | solution.py:25
  15.7 3.7 %subtract_convert_fusion = bf16[1024,1024]{1,0:T(8,128)(2,1)} fusion(f32[1024]{0:T(1024)S(1)} %broadcast_multiply_fusion.3, f32[1024]{0:T(1024)S(1)} %get-tuple-element.11, bf16[1024,1024]{1,0:T(8,128)(2,1)S(1)} %add_convert_fusion), kind=kOutput, calls=%fused_computation | convolution fusion | flops 2150629376 | bytes 4202496 | tf_op jit(solution)/shard_map/dot_general | solution.py:33
  20.2 9.5 %all-to-all-start = ((f32[32,2,1024]{2,1,0:T(2,128)}), f32[32,2,1024]{2,1,0:T(2,128)S(1)}, u32[]{:S(2)}, u32[]{:S(2)}) async-start(f32[32,2,1024]{2,1,0:T(2,128)} %broadcast_in_dim.28), calls=%async_computation | async-start | bytes 524288 | tf_op jit(solution)/shard_map/all_to_all | solution.py:86
  31.7 8.3 %collective-permute-done.1 = f32[1,1024]{1,0:T(1,128)S(1)} collective-permute-done((f32[1,1024]{1,0:T(1,128)S(1)}, f32[1,1024]{1,0:T(1,128)S(1)}, u32[]{:S(2)}, u32[]{:S(2)}) %collective-permute-start.1) | collective-permute-done | bytes 4128 | tf_op jit(solution)/shard_map/ppermute | solution.py:25
  40.1 3.6 %all-to-all-done = f32[32,2,1024]{2,1,0:T(2,128)S(1)} async-done(((f32[32,2,1024]{2,1,0:T(2,128)}), f32[32,2,1024]{2,1,0:T(2,128)S(1)}, u32[]{:S(2)}, u32[]{:S(2)}) %all-to-all-start) | async-done | bytes 262176 | tf_op jit(solution)/shard_map/all_to_all | solution.py:86
  43.9 4.0 %subtract_convert_fusion.1 = bf16[1024,1024]{1,0:T(8,128)(2,1)S(1)} fusion(f32[1024]{0:T(1024)S(1)} %bitcast.201, f32[1024]{0:T(1024)S(1)} %get-tuple-element.11, bf16[1024,1024]{1,0:T(8,128)(2,1)S(1)} %add_convert_fusion, bf16[1024,1024]{1,0:T(8,128)(2,1)} %collective-permute-done), kind=kOutput, calls=%fused_computation.1 | convolution fusion | flops 2150629376 | bytes 6299648 | tf_op jit(solution)/shard_map/dot_general | solution.py:33
  52.1 3.6 %collective-permute-done.6 = f32[33,1024]{1,0:T(8,128)S(1)} collective-permute-done((f32[33,1024]{1,0:T(8,128)S(1)}, f32[33,1024]{1,0:T(8,128)S(1)}, u32[]{:S(2)}, u32[]{:S(2)}) %collective-permute-start.6) | collective-permute-done | bytes 135200 | tf_op jit(solution)/shard_map/ppermute | solution.py:21
  59.8 3.6 %collective-permute-start.9 = (f32[65,1024]{1,0:T(8,128)S(1)}, f32[65,1024]{1,0:T(8,128)S(1)}, u32[]{:S(2)}, u32[]{:S(2)}) collective-permute-start(f32[65,1024]{1,0:T(8,128)S(1)} %pad_maximum_fusion.2), channel_id=1, source_target_pairs={{1,0},{2,1},{3,2},{5,4},{6,5},{7,6},{9,8},{10,9},{11,10},{13,12},{... | collective-permute-start | bytes 798728 | tf_op jit(solution)/shard_map/ppermute | solution.py:25
  63.5 5.9 %collective-permute-done.5 = bf16[2,128,1024]{2,1,0:T(8,128)(2,1)S(1)} collective-permute-done((bf16[2,128,1024]{2,1,0:T(8,128)(2,1)S(1)}, bf16[2,128,1024]{2,1,0:T(8,128)(2,1)S(1)}, u32[]{:S(2)}, u32[]{:S(2)}) %collective-permute-start.5) | collective-permute-done | bytes 524320 | tf_op jit(solution)/shard_map/ppermute | solution.py:21
  69.4 3.3 %collective-permute-done.3 = bf16[2,128,1024]{2,1,0:T(8,128)(2,1)S(1)} collective-permute-done((bf16[2,128,1024]{2,1,0:T(8,128)(2,1)S(1)}, bf16[2,128,1024]{2,1,0:T(8,128)(2,1)S(1)}, u32[]{:S(2)}, u32[]{:S(2)}) %collective-permute-start.3) | collective-permute-done | bytes 524320 | tf_op jit(solution)/shard_map/ppermute | solution.py:21
  73.9 3.4 %all-to-all-start.1 = ((bf16[8,16,1024]{2,1,0:T(8,128)(2,1)}), bf16[8,16,1024]{2,1,0:T(8,128)(2,1)S(1)}, u32[]{:S(2)}, u32[]{:S(2)}) async-start(bf16[8,16,1024]{2,1,0:T(8,128)(2,1)} %bitcast.179), calls=%async_computation.2 | async-start | bytes 524288 | tf_op jit(solution)/shard_map/all_to_all | solution.py:86
  77.4 6.0 %all-to-all-done.1 = bf16[8,16,1024]{2,1,0:T(8,128)(2,1)S(1)} async-done(((bf16[8,16,1024]{2,1,0:T(8,128)(2,1)}), bf16[8,16,1024]{2,1,0:T(8,128)(2,1)S(1)}, u32[]{:S(2)}, u32[]{:S(2)}) %all-to-all-start.1) | async-done | bytes 262176 | tf_op jit(solution)/shard_map/all_to_all | solution.py:86
  84.5 3.6 %all-to-all-start.2 = ((bf16[8,16,1024]{2,1,0:T(8,128)(2,1)}), bf16[8,16,1024]{2,1,0:T(8,128)(2,1)S(1)}, u32[]{:S(2)}, u32[]{:S(2)}) async-start(bf16[8,16,1024]{2,1,0:T(8,128)(2,1)} %broadcast_in_dim.30), calls=%async_computation.3 | async-start | bytes 524288 | tf_op jit(solution)/shard_map/all_to_all | solution.py:86
  88.3 5.9 %all-to-all-done.2 = bf16[8,16,1024]{2,1,0:T(8,128)(2,1)S(1)} async-done(((bf16[8,16,1024]{2,1,0:T(8,128)(2,1)}), bf16[8,16,1024]{2,1,0:T(8,128)(2,1)S(1)}, u32[]{:S(2)}, u32[]{:S(2)}) %all-to-all-start.2) | async-done | bytes 262176 | tf_op jit(solution)/shard_map/all_to_all | solution.py:86
  95.0 10.9 %reduce-scatter.5.cloned.1.call-done = bf16[32,1024]{1,0:T(8,128)(2,1)} async-done(((bf16[256,1024]{1,0:T(8,128)(2,1)}), bf16[32,1024]{1,0:T(8,128)(2,1)}) %reduce-scatter.5.cloned.1.call-update) | async-done | bytes 65552 | tf_op jit(solution)/shard_map/reduce_scatter | solution.py:154
  110.9 13.6 %all_to_all.25 = bf16[8,16,1024]{2,1,0:T(8,128)(2,1)S(1)} all-to-all(bf16[8,16,1024]{2,1,0:T(8,128)(2,1)S(1)} %broadcast_in_dim.61), channel_id=1, replica_groups=mesh['z'=8,'y'=4,'xl'=2,'xh'=2,'core'=2] {'z'}, dimensions={0} | all-to-all | bytes 524288 | tf_op jit(solution)/shard_map/all_to_all | solution.py:86
  126.1 5.0 %all-to-all-start.4 = ((bf16[8,128,1024]{2,1,0:T(8,128)(2,1)}), bf16[8,128,1024]{2,1,0:T(8,128)(2,1)S(1)}, u32[]{:S(2)}, u32[]{:S(2)}) async-start(bf16[8,128,1024]{2,1,0:T(8,128)(2,1)} %broadcast_in_dim.63), calls=%async_computation.6 | async-start | bytes 4194304 | tf_op jit(solution)/shard_map/all_to_all | solution.py:86
  131.1 12.2 %collective-permute-start.7 = (f32[16,1024]{1,0:T(8,128)S(1)}, f32[16,1024]{1,0:T(8,128)S(1)}, u32[]{:S(2)}, u32[]{:S(2)}) collective-permute-start(f32[16,1024]{1,0:T(8,128)S(1)} %get-tuple-element.44), channel_id=1, source_target_pairs={{1,0},{2,1},{3,2},{5,4},{6,5},{7,6},{9,8},{10,9},{11,10},{13,12},{... | collective-permute-start | bytes 196616 | tf_op jit(solution)/shard_map/ppermute | solution.py:25
  143.3 15.8 %collective-permute-done.7 = f32[16,1024]{1,0:T(8,128)S(1)} collective-permute-done((f32[16,1024]{1,0:T(8,128)S(1)}, f32[16,1024]{1,0:T(8,128)S(1)}, u32[]{:S(2)}, u32[]{:S(2)}) %collective-permute-start.7) | collective-permute-done | bytes 65568 | tf_op jit(solution)/shard_map/ppermute | solution.py:25
  159.6 5.0 %collective-permute-start.10 = (f32[16,1024]{1,0:T(8,128)S(1)}, f32[16,1024]{1,0:T(8,128)S(1)}, u32[]{:S(2)}, u32[]{:S(2)}) collective-permute-start(f32[16,1024]{1,0:T(8,128)S(1)} %slice_add_fusion.12), channel_id=1, source_target_pairs={{0,1},{1,2},{2,3},{4,5},{5,6},{6,7},{8,9},{9,10},{10,11},{12,13},{... | collective-permute-start | bytes 196616 | tf_op jit(solution)/shard_map/ppermute | solution.py:29
  173.8 5.1 %collective-permute-start.15 = (f32[16,1024]{1,0:T(8,128)S(1)}, f32[16,1024]{1,0:T(8,128)S(1)}, u32[]{:S(2)}, u32[]{:S(2)}) collective-permute-start(f32[16,1024]{1,0:T(8,128)S(1)} %slice_add_fusion.6), channel_id=1, source_target_pairs={{0,1},{1,2},{2,3},{4,5},{5,6},{6,7},{8,9},{9,10},{10,11},{12,13},{... | collective-permute-start | bytes 196616 | tf_op jit(solution)/shard_map/ppermute | solution.py:29
  181.0 3.6 %collective-permute-start.18 = (f32[7,16]{1,0:T(8,128)S(1)}, f32[7,16]{1,0:T(8,128)S(1)}, u32[]{:S(2)}, u32[]{:S(2)}) collective-permute-start(f32[7,16]{1,0:T(8,128)S(1)} %stack.61), channel_id=1, source_target_pairs={{0,3},{1,2},{2,1},{3,0},{4,7},{5,6},{6,5},{7,4},{8,11},{9,10},{10,... | collective-permute-start | bytes 1352 | tf_op jit(solution)/shard_map/ppermute | solution.py:205
  187.7 5.0 %collective-permute-start.20 = (f32[16,1024]{1,0:T(8,128)S(1)}, f32[16,1024]{1,0:T(8,128)S(1)}, u32[]{:S(2)}, u32[]{:S(2)}) collective-permute-start(f32[16,1024]{1,0:T(8,128)S(1)} %slice_add_fusion), channel_id=1, source_target_pairs={{0,1},{1,2},{2,3},{4,5},{5,6},{6,7},{8,9},{9,10},{10,11},{12,13},{... | collective-permute-start | bytes 196616 | tf_op jit(solution)/shard_map/ppermute | solution.py:29
  194.7 3.7 %collective-permute-start.23 = (f32[7,16]{1,0:T(8,128)S(1)}, f32[7,16]{1,0:T(8,128)S(1)}, u32[]{:S(2)}, u32[]{:S(2)}) collective-permute-start(f32[7,16]{1,0:T(8,128)S(1)} %stack.69), channel_id=1, source_target_pairs={{0,3},{1,2},{2,1},{3,0},{4,7},{5,6},{6,5},{7,4},{8,11},{9,10},{10,... | collective-permute-start | bytes 1352 | tf_op jit(solution)/shard_map/ppermute | solution.py:205
  (123 shorter events, 43.4 us)
Async XLA Ops:
  7.2 65.8 %reduce-scatter.3.cloned.1.call-start = ((), (), s32[]{:S(2)}) async-start(), calls=%async_computation.7 | async-start | bytes 2359296 | tf_op jit(solution)/shard_map/reduce_scatter | solution.py:137
  10.0 33.9 %collective-permute-start = (bf16[1024,1024]{1,0:T(8,128)(2,1)S(1)}, bf16[1024,1024]{1,0:T(8,128)(2,1)}, u32[]{:S(2)}, u32[]{:S(2)}) collective-permute-start(bf16[1024,1024]{1,0:T(8,128)(2,1)S(1)} %add_convert_fusion), channel_id=1, source_target_pairs={{1,0},{2,1},{3,2},{5,4},{6,5},{7,6},{9,8},{10,9},{11,10},{13,12},{... | collective-permute-start | bytes 6291464 | tf_op jit(solution)/shard_map/ppermute | solution.py:25
  20.2 23.5 %all-to-all-start = ((f32[32,2,1024]{2,1,0:T(2,128)}), f32[32,2,1024]{2,1,0:T(2,128)S(1)}, u32[]{:S(2)}, u32[]{:S(2)}) async-start(f32[32,2,1024]{2,1,0:T(2,128)} %broadcast_in_dim.28), calls=%async_computation | async-start | bytes 524288 | tf_op jit(solution)/shard_map/all_to_all | solution.py:86
  29.7 76.1 %reduce-scatter.5.cloned.1.call-start = ((), (), s32[]{:S(2)}) async-start(), calls=%async_computation.9 | async-start | bytes 589824 | tf_op jit(solution)/shard_map/reduce_scatter | solution.py:154
  29.8 10.3 %collective-permute-start.1 = (f32[1,1024]{1,0:T(1,128)S(1)}, f32[1,1024]{1,0:T(1,128)S(1)}, u32[]{:S(2)}, u32[]{:S(2)}) collective-permute-start(f32[1,1024]{1,0:T(1,128)S(1)} %bitcast.187), channel_id=1, source_target_pairs={{1,0},{2,1},{3,2},{5,4},{6,5},{7,6},{9,8},{10,9},{11,10},{13,12},{... | collective-permute-start | bytes 12296 | tf_op jit(solution)/shard_map/ppermute | solution.py:25
  48.0 8.7 %collective-permute-start.2 = (bf16[1,128,1024]{2,1,0:T(8,128)(2,1)S(1)}, bf16[1,128,1024]{2,1,0:T(8,128)(2,1)S(1)}, u32[]{:S(2)}, u32[]{:S(2)}) collective-permute-start(bf16[1,128,1024]{2,1,0:T(8,128)(2,1)S(1)} %get-tuple-element.53), channel_id=1, source_target_pairs={{0,8},{8,16},{16,24},{24,0},{1,9},{9,17},{17,25},{25,1},{2,10},{10... | collective-permute-start | bytes 786440 | tf_op jit(solution)/shard_map/ppermute | solution.py:21
  48.6 8.2 %collective-permute-start.4 = (bf16[1,128,1024]{2,1,0:T(8,128)(2,1)S(1)}, bf16[1,128,1024]{2,1,0:T(8,128)(2,1)S(1)}, u32[]{:S(2)}, u32[]{:S(2)}) collective-permute-start(bf16[1,128,1024]{2,1,0:T(8,128)(2,1)S(1)} %get-tuple-element.55), channel_id=1, source_target_pairs={{0,24},{8,0},{16,8},{24,16},{1,25},{9,1},{17,9},{25,17},{2,26},{10... | collective-permute-start | bytes 786440 | tf_op jit(solution)/shard_map/ppermute | solution.py:21
  57.0 12.4 %collective-permute-start.5 = (bf16[2,128,1024]{2,1,0:T(8,128)(2,1)S(1)}, bf16[2,128,1024]{2,1,0:T(8,128)(2,1)S(1)}, u32[]{:S(2)}, u32[]{:S(2)}) collective-permute-start(bf16[2,128,1024]{2,1,0:T(8,128)(2,1)S(1)} %pad_maximum_fusion.1), channel_id=1, source_target_pairs={{0,24},{8,0},{16,8},{24,16},{1,25},{9,1},{17,9},{25,17},{2,26},{10... | collective-permute-start | bytes 1572872 | tf_op jit(solution)/shard_map/ppermute | solution.py:21
  59.7 13.0 %collective-permute-start.3 = (bf16[2,128,1024]{2,1,0:T(8,128)(2,1)S(1)}, bf16[2,128,1024]{2,1,0:T(8,128)(2,1)S(1)}, u32[]{:S(2)}, u32[]{:S(2)}) collective-permute-start(bf16[2,128,1024]{2,1,0:T(8,128)(2,1)S(1)} %pad_maximum_fusion), channel_id=1, source_target_pairs={{0,8},{8,16},{16,24},{24,0},{1,9},{9,17},{17,25},{25,1},{2,10},{10... | collective-permute-start | bytes 1572872 | tf_op jit(solution)/shard_map/ppermute | solution.py:21
  59.8 28.4 %collective-permute-start.9 = (f32[65,1024]{1,0:T(8,128)S(1)}, f32[65,1024]{1,0:T(8,128)S(1)}, u32[]{:S(2)}, u32[]{:S(2)}) collective-permute-start(f32[65,1024]{1,0:T(8,128)S(1)} %pad_maximum_fusion.2), channel_id=1, source_target_pairs={{1,0},{2,1},{3,2},{5,4},{6,5},{7,6},{9,8},{10,9},{11,10},{13,12},{... | collective-permute-start | bytes 798728 | tf_op jit(solution)/shard_map/ppermute | solution.py:25
  73.9 9.5 %all-to-all-start.1 = ((bf16[8,16,1024]{2,1,0:T(8,128)(2,1)}), bf16[8,16,1024]{2,1,0:T(8,128)(2,1)S(1)}, u32[]{:S(2)}, u32[]{:S(2)}) async-start(bf16[8,16,1024]{2,1,0:T(8,128)(2,1)} %bitcast.179), calls=%async_computation.2 | async-start | bytes 524288 | tf_op jit(solution)/shard_map/all_to_all | solution.py:86
  84.5 9.7 %all-to-all-start.2 = ((bf16[8,16,1024]{2,1,0:T(8,128)(2,1)}), bf16[8,16,1024]{2,1,0:T(8,128)(2,1)S(1)}, u32[]{:S(2)}, u32[]{:S(2)}) async-start(bf16[8,16,1024]{2,1,0:T(8,128)(2,1)} %broadcast_in_dim.30), calls=%async_computation.3 | async-start | bytes 524288 | tf_op jit(solution)/shard_map/all_to_all | solution.py:86
  88.1 77.2 %all-gather.2.cloned.1.call-start = ((), (), s32[]{:S(2)}) async-start(), calls=%async_computation.8 | async-start | bytes 2359296 | tf_op jit(solution)/shard_map/all_gather | solution.py:190
  126.1 33.0 %all-to-all-start.4 = ((bf16[8,128,1024]{2,1,0:T(8,128)(2,1)}), bf16[8,128,1024]{2,1,0:T(8,128)(2,1)S(1)}, u32[]{:S(2)}, u32[]{:S(2)}) async-start(bf16[8,128,1024]{2,1,0:T(8,128)(2,1)} %broadcast_in_dim.63), calls=%async_computation.6 | async-start | bytes 4194304 | tf_op jit(solution)/shard_map/all_to_all | solution.py:86
  131.1 28.0 %collective-permute-start.7 = (f32[16,1024]{1,0:T(8,128)S(1)}, f32[16,1024]{1,0:T(8,128)S(1)}, u32[]{:S(2)}, u32[]{:S(2)}) collective-permute-start(f32[16,1024]{1,0:T(8,128)S(1)} %get-tuple-element.44), channel_id=1, source_target_pairs={{1,0},{2,1},{3,2},{5,4},{6,5},{7,6},{9,8},{10,9},{11,10},{13,12},{... | collective-permute-start | bytes 196616 | tf_op jit(solution)/shard_map/ppermute | solution.py:25
  159.6 8.1 %collective-permute-start.10 = (f32[16,1024]{1,0:T(8,128)S(1)}, f32[16,1024]{1,0:T(8,128)S(1)}, u32[]{:S(2)}, u32[]{:S(2)}) collective-permute-start(f32[16,1024]{1,0:T(8,128)S(1)} %slice_add_fusion.12), channel_id=1, source_target_pairs={{0,1},{1,2},{2,3},{4,5},{5,6},{6,7},{8,9},{9,10},{10,11},{12,13},{... | collective-permute-start | bytes 196616 | tf_op jit(solution)/shard_map/ppermute | solution.py:29
  167.9 11.8 %collective-permute-start.12 = (f32[2,16]{1,0:T(2,128)S(1)}, f32[2,16]{1,0:T(2,128)S(1)}, u32[]{:S(2)}, u32[]{:S(2)}) collective-permute-start(f32[2,16]{1,0:T(2,128)S(1)} %pad_maximum_fusion.14), channel_id=1, source_target_pairs={{0,2},{2,0},{1,3},{3,1},{4,6},{6,4},{5,7},{7,5},{8,10},{10,8},{9,1... | collective-permute-start | bytes 392 | tf_op jit(solution)/shard_map/ppermute | solution.py:21
  168.0 11.7 %collective-permute-start.13 = (f32[2,16]{1,0:T(2,128)S(1)}, f32[2,16]{1,0:T(2,128)S(1)}, u32[]{:S(2)}, u32[]{:S(2)}) collective-permute-start(f32[2,16]{1,0:T(2,128)S(1)} %pad_maximum_fusion.14), channel_id=1, source_target_pairs={{0,3},{1,2},{2,1},{3,0},{4,7},{5,6},{6,5},{7,4},{8,11},{9,10},{10,... | collective-permute-start | bytes 392 | tf_op jit(solution)/shard_map/ppermute | solution.py:205
  170.2 9.6 %collective-permute-start.11 = (f32[2,16]{1,0:T(2,128)S(1)}, f32[2,16]{1,0:T(2,128)S(1)}, u32[]{:S(2)}, u32[]{:S(2)}) collective-permute-start(f32[2,16]{1,0:T(2,128)S(1)} %pad_maximum_fusion.14), channel_id=1, source_target_pairs={{0,1},{1,0},{2,3},{3,2},{4,5},{5,4},{6,7},{7,6},{8,9},{9,8},{10,11... | collective-permute-start | bytes 392 | tf_op jit(solution)/shard_map/ppermute | solution.py:21
  171.4 8.4 %collective-permute-start.14 = (f32[16,1024]{1,0:T(8,128)S(1)}, f32[16,1024]{1,0:T(8,128)S(1)}, u32[]{:S(2)}, u32[]{:S(2)}) collective-permute-start(f32[16,1024]{1,0:T(8,128)S(1)} %get-tuple-element.41), channel_id=1, source_target_pairs={{1,0},{2,1},{3,2},{5,4},{6,5},{7,6},{9,8},{10,9},{11,10},{13,12},{... | collective-permute-start | bytes 196616 | tf_op jit(solution)/shard_map/ppermute | solution.py:25
  173.8 6.8 %collective-permute-start.15 = (f32[16,1024]{1,0:T(8,128)S(1)}, f32[16,1024]{1,0:T(8,128)S(1)}, u32[]{:S(2)}, u32[]{:S(2)}) collective-permute-start(f32[16,1024]{1,0:T(8,128)S(1)} %slice_add_fusion.6), channel_id=1, source_target_pairs={{0,1},{1,2},{2,3},{4,5},{5,6},{6,7},{8,9},{9,10},{10,11},{12,13},{... | collective-permute-start | bytes 196616 | tf_op jit(solution)/shard_map/ppermute | solution.py:29
  180.9 6.2 %collective-permute-start.17 = (f32[7,16]{1,0:T(8,128)S(1)}, f32[7,16]{1,0:T(8,128)S(1)}, u32[]{:S(2)}, u32[]{:S(2)}) collective-permute-start(f32[7,16]{1,0:T(8,128)S(1)} %stack.61), channel_id=1, source_target_pairs={{0,2},{2,0},{1,3},{3,1},{4,6},{6,4},{5,7},{7,5},{8,10},{10,8},{9,1... | collective-permute-start | bytes 1352 | tf_op jit(solution)/shard_map/ppermute | solution.py:21
  185.0 8.5 %collective-permute-start.19 = (f32[16,1024]{1,0:T(8,128)S(1)}, f32[16,1024]{1,0:T(8,128)S(1)}, u32[]{:S(2)}, u32[]{:S(2)}) collective-permute-start(f32[16,1024]{1,0:T(8,128)S(1)} %get-tuple-element.35), channel_id=1, source_target_pairs={{1,0},{2,1},{3,2},{5,4},{6,5},{7,6},{9,8},{10,9},{11,10},{13,12},{... | collective-permute-start | bytes 196616 | tf_op jit(solution)/shard_map/ppermute | solution.py:25
  187.7 6.5 %collective-permute-start.20 = (f32[16,1024]{1,0:T(8,128)S(1)}, f32[16,1024]{1,0:T(8,128)S(1)}, u32[]{:S(2)}, u32[]{:S(2)}) collective-permute-start(f32[16,1024]{1,0:T(8,128)S(1)} %slice_add_fusion), channel_id=1, source_target_pairs={{0,1},{1,2},{2,3},{4,5},{5,6},{6,7},{8,9},{9,10},{10,11},{12,13},{... | collective-permute-start | bytes 196616 | tf_op jit(solution)/shard_map/ppermute | solution.py:29
  (12 other events, 61.0 us)
Sparse Core Ops, SparseCore 0:
  19.6 42.7 reduce-scatter.2
  74.0 31.8 reduce-scatter.4
  107.7 43.0 all-gather.1
where the time goes:
time: 209 us; the launch traced here: 207 us
  starting transfers between devices  83 us (40%)
  waiting for transfers between devices  67.7 us (32%)
  matrix products  16.6 us (8%)
  between operations  14.4 us (7%)
  blocking collectives  13.6 us (7%)
  other arithmetic  6.37 us (3%)
  local copies, waits for them, and re-layouts  5.62 us (3%)
    ppermute x6, starting transfers between devices, from_next(): lax.ppermute(block, BLOCK_AXES, [(i + 1, i) for i in range(N_BLOCKS - 1)])  26.9 us
    ppermute x6, waiting for transfers between devices, from_next(): lax.ppermute(block, BLOCK_AXES, [(i + 1, i) for i in range(N_BLOCKS - 1)])  24.1 us
    all_to_all x4, starting transfers between devices, exchange(): return lax.all_to_all(parts, axes, 0, 0, tiled=True)  21.5 us
    ppermute x12, waiting for transfers between devices, shift(): lax.ppermute(block, axis, [(i, (i + distance) % size) for i in range(size)])  15.8 us
    all_to_all x4, waiting for transfers between devices, exchange(): return lax.all_to_all(parts, axes, 0, 0, tiled=True)  15.6 us
    ppermute x3, starting transfers between devices, from_previous(): lax.ppermute(block, BLOCK_AXES, [(i, i + 1) for i in range(N_BLOCKS - 1)])  15.1 us
    all_to_all x1, blocking collectives, exchange(): return lax.all_to_all(parts, axes, 0, 0, tiled=True)  13.6 us
    reduce_scatter x1, waiting for transfers between devices, on_device(): edge_sum = lax.psum_scatter(edge_sum, 'z', scatter_dimension=0, tiled=True)  10.9 us
  transfers between devices with their start and end apart: 31, of which 12 were waited for; matrix products, arithmetic and copies ran while one was open for 11% of the time, Pallas kernels for 0%

commit v1 on v0

--- a/solution.py
+++ b/solution.py
@@ -149,9 +149,9 @@
     n_place, n_row = lax.axis_size("z"), lax.axis_size("y")
     edge_part = edge_part.reshape(n_row, 2, -1, width).swapaxes(0, 1)
     edge_sum = ring_reduce(edge_part, "y").astype(BF16)
+    edge_sum = edge_sum.reshape(2, n_place, -1, width).swapaxes(0, 1).reshape(-1, width)
+    edge_sum = reduce_over(edge_sum, "z").astype(BF16)
     edge_sum, own_sum = lax.optimization_barrier((edge_sum, own_sum))
-    edge_sum = edge_sum.reshape(2, n_place, -1, width).swapaxes(0, 1).reshape(-1, width)
-    edge_sum = lax.psum_scatter(edge_sum, "z", scatter_dimension=0, tiled=True)
     edge_sum = edge_sum.reshape(2, -1, width)
     side = lax.axis_index("xl").astype(jnp.uint32)
     kept = lax.dynamic_index_in_dim(edge_sum, side, 0, keepdims=False)
@@ -200,10 +200,8 @@
 
     def dots(*pairs):
         local = jnp.stack([jnp.sum(a * b, axis=1) for a, b in pairs])
-        opposite = [(i, N_BLOCKS - 1 - i) for i in range(N_BLOCKS)]
-        near, far = shift(local, "core", 1), shift(local, "xh", 1)
-        across = lax.ppermute(local, BLOCK_AXES, opposite)
-        return ((local + near) + (far + across))[:, :, None]
+        local = local + shift(local, "core", 1)
+        return (local + shift(local, "xh", 1))[:, :, None]
 
     mask = typed_mask[None, :]
     mask_row = mask.astype(F32)

time: 209 us -> 211 us (level)
  waiting for transfers between devices: 67.7 us -> 76.7 us
  starting transfers between devices: 83 us -> 78 us
    ppermute x12, waiting for transfers between devices: 15.8 us -> 28.3 us  [shift(): lax.ppermute(block, axis, [(i, (i + distance) % size) for i in range(size)])]
    reduce_scatter x1 -> x0, waiting for transfers between devices: 10.9 us -> none  [on_device(): edge_sum = lax.psum_scatter(edge_sum, 'z', scatter_dimension=0, tiled=True)]
    ppermute x3 -> x0, starting transfers between devices: 9.45 us -> none  [dots(): across = lax.ppermute(local, BLOCK_AXES, opposite)]
    all_to_all x4 -> x5, waiting for transfers between devices: 15.6 us -> 24.3 us  [exchange(): return lax.all_to_all(parts, axes, 0, 0, tiled=True)]
    ppermute x12, starting transfers between devices: 9.95 us -> 12.9 us  [shift(): lax.ppermute(block, axis, [(i, (i + distance) % size) for i in range(size)])]
    all_to_all x4 -> x5, starting transfers between devices: 21.5 us -> 23.7 us  [exchange(): return lax.all_to_all(parts, axes, 0, 0, tiled=True)]
  transfers between devices with their start and end apart: 31 -> 28, of which waited for: 12 -> 13; matrix products, arithmetic and copies ran while one was open for 11% -> 11% of each run, Pallas kernels for 0% -> 0%
where the time goes in v1:
time: 211 us; the launch traced here: 210 us
  starting transfers between devices  78 us (37%)
  waiting for transfers between devices  76.7 us (36%)
  matrix products  15.9 us (8%)
  between operations  14.7 us (7%)
  blocking collectives  11.8 us (6%)
  other arithmetic  7.5 us (4%)
  local copies, waits for them, and re-layouts  4.87 us (2%)
    ppermute x12, waiting for transfers between devices, shift(): lax.ppermute(block, axis, [(i, (i + distance) % size) for i in range(size)])  28.3 us
    ppermute x6, starting transfers between devices, from_next(): lax.ppermute(block, BLOCK_AXES, [(i + 1, i) for i in range(N_BLOCKS - 1)])  26.3 us
    all_to_all x5, waiting for transfers between devices, exchange(): return lax.all_to_all(parts, axes, 0, 0, tiled=True)  24.3 us
    ppermute x6, waiting for transfers between devices, from_next(): lax.ppermute(block, BLOCK_AXES, [(i + 1, i) for i in range(N_BLOCKS - 1)])  24.2 us
    all_to_all x5, starting transfers between devices, exchange(): return lax.all_to_all(parts, axes, 0, 0, tiled=True)  23.7 us
    ppermute x3, starting transfers between devices, from_previous(): lax.ppermute(block, BLOCK_AXES, [(i, i + 1) for i in range(N_BLOCKS - 1)])  15 us
    ppermute x12, starting transfers between devices, shift(): lax.ppermute(block, axis, [(i, (i + distance) % size) for i in range(size)])  12.9 us
    all_to_all x1, blocking collectives, exchange(): return lax.all_to_all(parts, axes, 0, 0, tiled=True)  11.8 us
  transfers between devices with their start and end apart: 28, of which 13 were waited for; matrix products, arithmetic and copies ran while one was open for 11% of the time, Pallas kernels for 0%

profile of v1, /device:TPU:1, one launch (start us, length us, event | category | flops | bytes accessed | tf_op | source)
XLA Modules:
  0.0 209.6 jit_solution(8761730430510721017)
XLA Ops:
  9.9 5.1 %collective-permute-start = (bf16[1024,1024]{1,0:T(8,128)(2,1)S(1)}, bf16[1024,1024]{1,0:T(8,128)(2,1)}, u32[]{:S(2)}, u32[]{:S(2)}) collective-permute-start(bf16[1024,1024]{1,0:T(8,128)(2,1)S(1)} %add_convert_fusion), channel_id=1, source_target_pairs={{1,0},{2,1},{3,2},{5,4},{6,5},{7,6},{9,8},{10,9},{11,10},{13,12},{... | collective-permute-start | bytes 6291464 | tf_op jit(solution)/shard_map/ppermute | solution.py:25
  16.5 9.5 %all-to-all-start = ((f32[32,2,1024]{2,1,0:T(2,128)}), f32[32,2,1024]{2,1,0:T(2,128)S(1)}, u32[]{:S(2)}, u32[]{:S(2)}) async-start(f32[32,2,1024]{2,1,0:T(2,128)} %broadcast_in_dim.28), calls=%async_computation | async-start | bytes 524288 | tf_op jit(solution)/shard_map/all_to_all | solution.py:86
  26.0 3.7 %subtract_convert_fusion = bf16[1024,1024]{1,0:T(8,128)(2,1)} fusion(f32[1024]{0:T(1024)S(1)} %broadcast_multiply_fusion.3, f32[1024]{0:T(1024)S(1)} %get-tuple-element.11, bf16[1024,1024]{1,0:T(8,128)(2,1)S(1)} %add_convert_fusion), kind=kOutput, calls=%fused_computation | convolution fusion | flops 2150629376 | bytes 4202496 | tf_op jit(solution)/shard_map/dot_general | solution.py:33
  31.7 8.1 %collective-permute-done.1 = f32[1,1024]{1,0:T(1,128)S(1)} collective-permute-done((f32[1,1024]{1,0:T(1,128)S(1)}, f32[1,1024]{1,0:T(1,128)S(1)}, u32[]{:S(2)}, u32[]{:S(2)}) %collective-permute-start.1) | collective-permute-done | bytes 4128 | tf_op jit(solution)/shard_map/ppermute | solution.py:25
  40.1 4.0 %subtract_convert_fusion.1 = bf16[1024,1024]{1,0:T(8,128)(2,1)S(1)} fusion(f32[1024]{0:T(1024)S(1)} %bitcast.202, f32[1024]{0:T(1024)S(1)} %get-tuple-element.11, bf16[1024,1024]{1,0:T(8,128)(2,1)S(1)} %add_convert_fusion, bf16[1024,1024]{1,0:T(8,128)(2,1)} %collective-permute-done), kind=kOutput, calls=%fused_computation.1 | convolution fusion | flops 2150629376 | bytes 6299648 | tf_op jit(solution)/shard_map/dot_general | solution.py:33
  47.1 6.6 %collective-permute-done.2 = bf16[1,128,1024]{2,1,0:T(8,128)(2,1)S(1)} collective-permute-done((bf16[1,128,1024]{2,1,0:T(8,128)(2,1)S(1)}, bf16[1,128,1024]{2,1,0:T(8,128)(2,1)S(1)}, u32[]{:S(2)}, u32[]{:S(2)}) %collective-permute-start.2) | collective-permute-done | bytes 262176 | tf_op jit(solution)/shard_map/ppermute | solution.py:21
  58.2 9.4 %collective-permute-done.5 = bf16[2,128,1024]{2,1,0:T(8,128)(2,1)S(1)} collective-permute-done((bf16[2,128,1024]{2,1,0:T(8,128)(2,1)S(1)}, bf16[2,128,1024]{2,1,0:T(8,128)(2,1)S(1)}, u32[]{:S(2)}, u32[]{:S(2)}) %collective-permute-start.5) | collective-permute-done | bytes 524320 | tf_op jit(solution)/shard_map/ppermute | solution.py:21
  67.6 3.3 %collective-permute-done.3 = bf16[2,128,1024]{2,1,0:T(8,128)(2,1)S(1)} collective-permute-done((bf16[2,128,1024]{2,1,0:T(8,128)(2,1)S(1)}, bf16[2,128,1024]{2,1,0:T(8,128)(2,1)S(1)}, u32[]{:S(2)}, u32[]{:S(2)}) %collective-permute-start.3) | collective-permute-done | bytes 524320 | tf_op jit(solution)/shard_map/ppermute | solution.py:21
  73.0 3.5 %all-to-all-start.1 = ((bf16[8,32,1024]{2,1,0:T(8,128)(2,1)}), bf16[8,32,1024]{2,1,0:T(8,128)(2,1)S(1)}, u32[]{:S(2)}, u32[]{:S(2)}) async-start(bf16[8,32,1024]{2,1,0:T(8,128)(2,1)} %bitcast.15), calls=%async_computation.1 | async-start | bytes 1048576 | tf_op jit(solution)/shard_map/all_to_all | solution.py:86
  76.7 3.5 %collective-permute-start.9 = (f32[65,1024]{1,0:T(8,128)S(1)}, f32[65,1024]{1,0:T(8,128)S(1)}, u32[]{:S(2)}, u32[]{:S(2)}) collective-permute-start(f32[65,1024]{1,0:T(8,128)S(1)} %pad_maximum_fusion.2), channel_id=1, source_target_pairs={{1,0},{2,1},{3,2},{5,4},{6,5},{7,6},{9,8},{10,9},{11,10},{13,12},{... | collective-permute-start | bytes 798728 | tf_op jit(solution)/shard_map/ppermute | solution.py:25
  80.4 12.4 %all-to-all-done.1 = bf16[8,32,1024]{2,1,0:T(8,128)(2,1)S(1)} async-done(((bf16[8,32,1024]{2,1,0:T(8,128)(2,1)}), bf16[8,32,1024]{2,1,0:T(8,128)(2,1)S(1)}, u32[]{:S(2)}, u32[]{:S(2)}) %all-to-all-start.1) | async-done | bytes 524320 | tf_op jit(solution)/shard_map/all_to_all | solution.py:86
  92.9 3.6 %all-to-all-start.2 = ((bf16[8,16,1024]{2,1,0:T(8,128)(2,1)}), bf16[8,16,1024]{2,1,0:T(8,128)(2,1)S(1)}, u32[]{:S(2)}, u32[]{:S(2)}) async-start(bf16[8,16,1024]{2,1,0:T(8,128)(2,1)} %bitcast.178), calls=%async_computation.3 | async-start | bytes 524288 | tf_op jit(solution)/shard_map/all_to_all | solution.py:86
  96.6 5.9 %all-to-all-done.2 = bf16[8,16,1024]{2,1,0:T(8,128)(2,1)S(1)} async-done(((bf16[8,16,1024]{2,1,0:T(8,128)(2,1)}), bf16[8,16,1024]{2,1,0:T(8,128)(2,1)S(1)}, u32[]{:S(2)}, u32[]{:S(2)}) %all-to-all-start.2) | async-done | bytes 262176 | tf_op jit(solution)/shard_map/all_to_all | solution.py:86
  103.6 3.4 %all-to-all-start.3 = ((bf16[8,16,1024]{2,1,0:T(8,128)(2,1)}), bf16[8,16,1024]{2,1,0:T(8,128)(2,1)S(1)}, u32[]{:S(2)}, u32[]{:S(2)}) async-start(bf16[8,16,1024]{2,1,0:T(8,128)(2,1)} %broadcast_in_dim.30), calls=%async_computation.4 | async-start | bytes 524288 | tf_op jit(solution)/shard_map/all_to_all | solution.py:86
  107.2 5.9 %all-to-all-done.3 = bf16[8,16,1024]{2,1,0:T(8,128)(2,1)S(1)} async-done(((bf16[8,16,1024]{2,1,0:T(8,128)(2,1)}), bf16[8,16,1024]{2,1,0:T(8,128)(2,1)S(1)}, u32[]{:S(2)}, u32[]{:S(2)}) %all-to-all-start.3) | async-done | bytes 262176 | tf_op jit(solution)/shard_map/all_to_all | solution.py:86
  117.4 11.8 %all_to_all.30 = bf16[8,16,1024]{2,1,0:T(8,128)(2,1)S(1)} all-to-all(bf16[8,16,1024]{2,1,0:T(8,128)(2,1)S(1)} %broadcast_in_dim.61), channel_id=1, replica_groups=mesh['z'=8,'y'=4,'xl'=2,'xh'=2,'core'=2] {'z'}, dimensions={0} | all-to-all | bytes 524288 | tf_op jit(solution)/shard_map/all_to_all | solution.py:86
  130.8 3.7 %all-to-all-start.5 = ((bf16[8,128,1024]{2,1,0:T(8,128)(2,1)}), bf16[8,128,1024]{2,1,0:T(8,128)(2,1)S(1)}, u32[]{:S(2)}, u32[]{:S(2)}) async-start(bf16[8,128,1024]{2,1,0:T(8,128)(2,1)} %broadcast_in_dim.63), calls=%async_computation.6 | async-start | bytes 4194304 | tf_op jit(solution)/shard_map/all_to_all | solution.py:86
  134.6 11.1 %collective-permute-start.7 = (f32[16,1024]{1,0:T(8,128)S(1)}, f32[16,1024]{1,0:T(8,128)S(1)}, u32[]{:S(2)}, u32[]{:S(2)}) collective-permute-start(f32[16,1024]{1,0:T(8,128)S(1)} %get-tuple-element.44), channel_id=1, source_target_pairs={{1,0},{2,1},{3,2},{5,4},{6,5},{7,6},{9,8},{10,9},{11,10},{13,12},{... | collective-permute-start | bytes 196616 | tf_op jit(solution)/shard_map/ppermute | solution.py:25
  145.8 16.1 %collective-permute-done.7 = f32[16,1024]{1,0:T(8,128)S(1)} collective-permute-done((f32[16,1024]{1,0:T(8,128)S(1)}, f32[16,1024]{1,0:T(8,128)S(1)}, u32[]{:S(2)}, u32[]{:S(2)}) %collective-permute-start.7) | collective-permute-done | bytes 65568 | tf_op jit(solution)/shard_map/ppermute | solution.py:25
  162.4 5.1 %collective-permute-start.10 = (f32[16,1024]{1,0:T(8,128)S(1)}, f32[16,1024]{1,0:T(8,128)S(1)}, u32[]{:S(2)}, u32[]{:S(2)}) collective-permute-start(f32[16,1024]{1,0:T(8,128)S(1)} %slice_add_fusion.12), channel_id=1, source_target_pairs={{0,1},{1,2},{2,3},{4,5},{5,6},{6,7},{8,9},{9,10},{10,11},{12,13},{... | collective-permute-start | bytes 196616 | tf_op jit(solution)/shard_map/ppermute | solution.py:29
  173.5 5.1 %collective-permute-start.14 = (f32[16,1024]{1,0:T(8,128)S(1)}, f32[16,1024]{1,0:T(8,128)S(1)}, u32[]{:S(2)}, u32[]{:S(2)}) collective-permute-start(f32[16,1024]{1,0:T(8,128)S(1)} %slice_add_fusion.6), channel_id=1, source_target_pairs={{0,1},{1,2},{2,3},{4,5},{5,6},{6,7},{8,9},{9,10},{10,11},{12,13},{... | collective-permute-start | bytes 196616 | tf_op jit(solution)/shard_map/ppermute | solution.py:29
  179.6 3.2 %collective-permute-done.12 = f32[2,16]{1,0:T(2,128)S(1)} collective-permute-done((f32[2,16]{1,0:T(2,128)S(1)}, f32[2,16]{1,0:T(2,128)S(1)}, u32[]{:S(2)}, u32[]{:S(2)}) %collective-permute-start.12) | collective-permute-done | bytes 160 | tf_op jit(solution)/shard_map/ppermute | solution.py:21
  189.7 4.7 %collective-permute-start.18 = (f32[16,1024]{1,0:T(8,128)S(1)}, f32[16,1024]{1,0:T(8,128)S(1)}, u32[]{:S(2)}, u32[]{:S(2)}) collective-permute-start(f32[16,1024]{1,0:T(8,128)S(1)} %slice_add_fusion), channel_id=1, source_target_pairs={{0,1},{1,2},{2,3},{4,5},{5,6},{6,7},{8,9},{9,10},{10,11},{12,13},{... | collective-permute-start | bytes 196616 | tf_op jit(solution)/shard_map/ppermute | solution.py:29
  197.6 3.4 %collective-permute-start.20 = (f32[7,16]{1,0:T(8,128)S(1)}, f32[7,16]{1,0:T(8,128)S(1)}, u32[]{:S(2)}, u32[]{:S(2)}) collective-permute-start(f32[7,16]{1,0:T(8,128)S(1)} %add.467), channel_id=1, source_target_pairs={{0,2},{2,0},{1,3},{3,1},{4,6},{6,4},{5,7},{7,5},{8,10},{10,8},{9,1... | collective-permute-start | bytes 1352 | tf_op jit(solution)/shard_map/ppermute | solution.py:21
  (122 shorter events, 42.5 us)
Async XLA Ops:
  9.9 30.1 %collective-permute-start = (bf16[1024,1024]{1,0:T(8,128)(2,1)S(1)}, bf16[1024,1024]{1,0:T(8,128)(2,1)}, u32[]{:S(2)}, u32[]{:S(2)}) collective-permute-start(bf16[1024,1024]{1,0:T(8,128)(2,1)S(1)} %add_convert_fusion), channel_id=1, source_target_pairs={{1,0},{2,1},{3,2},{5,4},{6,5},{7,6},{9,8},{10,9},{11,10},{13,12},{... | collective-permute-start | bytes 6291464 | tf_op jit(solution)/shard_map/ppermute | solution.py:25
  16.5 23.3 %all-to-all-start = ((f32[32,2,1024]{2,1,0:T(2,128)}), f32[32,2,1024]{2,1,0:T(2,128)S(1)}, u32[]{:S(2)}, u32[]{:S(2)}) async-start(f32[32,2,1024]{2,1,0:T(2,128)} %broadcast_in_dim.28), calls=%async_computation | async-start | bytes 524288 | tf_op jit(solution)/shard_map/all_to_all | solution.py:86
  26.0 67.0 %reduce-scatter.2.cloned.1.call-start = ((), (), s32[]{:S(2)}) async-start(), calls=%async_computation.7 | async-start | bytes 2359296 | tf_op jit(solution)/shard_map/reduce_scatter | solution.py:137
  29.8 10.0 %collective-permute-start.1 = (f32[1,1024]{1,0:T(1,128)S(1)}, f32[1,1024]{1,0:T(1,128)S(1)}, u32[]{:S(2)}, u32[]{:S(2)}) collective-permute-start(f32[1,1024]{1,0:T(1,128)S(1)} %bitcast.186), channel_id=1, source_target_pairs={{1,0},{2,1},{3,2},{5,4},{6,5},{7,6},{9,8},{10,9},{11,10},{13,12},{... | collective-permute-start | bytes 12296 | tf_op jit(solution)/shard_map/ppermute | solution.py:25
  44.2 9.5 %collective-permute-start.2 = (bf16[1,128,1024]{2,1,0:T(8,128)(2,1)S(1)}, bf16[1,128,1024]{2,1,0:T(8,128)(2,1)S(1)}, u32[]{:S(2)}, u32[]{:S(2)}) collective-permute-start(bf16[1,128,1024]{2,1,0:T(8,128)(2,1)S(1)} %get-tuple-element.53), channel_id=1, source_target_pairs={{0,8},{8,16},{16,24},{24,0},{1,9},{9,17},{17,25},{25,1},{2,10},{10... | collective-permute-start | bytes 786440 | tf_op jit(solution)/shard_map/ppermute | solution.py:21
  45.5 8.1 %collective-permute-start.4 = (bf16[1,128,1024]{2,1,0:T(8,128)(2,1)S(1)}, bf16[1,128,1024]{2,1,0:T(8,128)(2,1)S(1)}, u32[]{:S(2)}, u32[]{:S(2)}) collective-permute-start(bf16[1,128,1024]{2,1,0:T(8,128)(2,1)S(1)} %get-tuple-element.55), channel_id=1, source_target_pairs={{0,24},{8,0},{16,8},{24,16},{1,25},{9,1},{17,9},{25,17},{2,26},{10... | collective-permute-start | bytes 786440 | tf_op jit(solution)/shard_map/ppermute | solution.py:21
  53.9 13.7 %collective-permute-start.5 = (bf16[2,128,1024]{2,1,0:T(8,128)(2,1)S(1)}, bf16[2,128,1024]{2,1,0:T(8,128)(2,1)S(1)}, u32[]{:S(2)}, u32[]{:S(2)}) collective-permute-start(bf16[2,128,1024]{2,1,0:T(8,128)(2,1)S(1)} %pad_maximum_fusion.1), channel_id=1, source_target_pairs={{0,24},{8,0},{16,8},{24,16},{1,25},{9,1},{17,9},{25,17},{2,26},{10... | collective-permute-start | bytes 1572872 | tf_op jit(solution)/shard_map/ppermute | solution.py:21
  56.9 14.0 %collective-permute-start.3 = (bf16[2,128,1024]{2,1,0:T(8,128)(2,1)S(1)}, bf16[2,128,1024]{2,1,0:T(8,128)(2,1)S(1)}, u32[]{:S(2)}, u32[]{:S(2)}) collective-permute-start(bf16[2,128,1024]{2,1,0:T(8,128)(2,1)S(1)} %pad_maximum_fusion), channel_id=1, source_target_pairs={{0,8},{8,16},{16,24},{24,0},{1,9},{9,17},{17,25},{25,1},{2,10},{10... | collective-permute-start | bytes 1572872 | tf_op jit(solution)/shard_map/ppermute | solution.py:21
  57.0 19.5 %collective-permute-start.6 = (f32[33,1024]{1,0:T(8,128)S(1)}, f32[33,1024]{1,0:T(8,128)S(1)}, u32[]{:S(2)}, u32[]{:S(2)}) collective-permute-start(f32[33,1024]{1,0:T(8,128)S(1)} %pad_maximum_fusion.3), channel_id=1, source_target_pairs={{0,4},{4,0},{1,5},{5,1},{2,6},{6,2},{3,7},{7,3},{8,12},{12,8},{9,1... | collective-permute-start | bytes 405512 | tf_op jit(solution)/shard_map/ppermute | solution.py:21
  73.0 19.8 %all-to-all-start.1 = ((bf16[8,32,1024]{2,1,0:T(8,128)(2,1)}), bf16[8,32,1024]{2,1,0:T(8,128)(2,1)S(1)}, u32[]{:S(2)}, u32[]{:S(2)}) async-start(bf16[8,32,1024]{2,1,0:T(8,128)(2,1)} %bitcast.15), calls=%async_computation.1 | async-start | bytes 1048576 | tf_op jit(solution)/shard_map/all_to_all | solution.py:86
  76.7 30.4 %collective-permute-start.9 = (f32[65,1024]{1,0:T(8,128)S(1)}, f32[65,1024]{1,0:T(8,128)S(1)}, u32[]{:S(2)}, u32[]{:S(2)}) collective-permute-start(f32[65,1024]{1,0:T(8,128)S(1)} %pad_maximum_fusion.2), channel_id=1, source_target_pairs={{1,0},{2,1},{3,2},{5,4},{6,5},{7,6},{9,8},{10,9},{11,10},{13,12},{... | collective-permute-start | bytes 798728 | tf_op jit(solution)/shard_map/ppermute | solution.py:25
  92.9 9.5 %all-to-all-start.2 = ((bf16[8,16,1024]{2,1,0:T(8,128)(2,1)}), bf16[8,16,1024]{2,1,0:T(8,128)(2,1)S(1)}, u32[]{:S(2)}, u32[]{:S(2)}) async-start(bf16[8,16,1024]{2,1,0:T(8,128)(2,1)} %bitcast.178), calls=%async_computation.3 | async-start | bytes 524288 | tf_op jit(solution)/shard_map/all_to_all | solution.py:86
  103.6 9.5 %all-to-all-start.3 = ((bf16[8,16,1024]{2,1,0:T(8,128)(2,1)}), bf16[8,16,1024]{2,1,0:T(8,128)(2,1)S(1)}, u32[]{:S(2)}, u32[]{:S(2)}) async-start(bf16[8,16,1024]{2,1,0:T(8,128)(2,1)} %broadcast_in_dim.30), calls=%async_computation.4 | async-start | bytes 524288 | tf_op jit(solution)/shard_map/all_to_all | solution.py:86
  107.0 61.3 %all-gather.2.cloned.1.call-start = ((), (), s32[]{:S(2)}) async-start(), calls=%async_computation.8 | async-start | bytes 2359296 | tf_op jit(solution)/shard_map/all_gather | solution.py:190
  130.8 31.1 %all-to-all-start.5 = ((bf16[8,128,1024]{2,1,0:T(8,128)(2,1)}), bf16[8,128,1024]{2,1,0:T(8,128)(2,1)S(1)}, u32[]{:S(2)}, u32[]{:S(2)}) async-start(bf16[8,128,1024]{2,1,0:T(8,128)(2,1)} %broadcast_in_dim.63), calls=%async_computation.6 | async-start | bytes 4194304 | tf_op jit(solution)/shard_map/all_to_all | solution.py:86
  134.6 27.2 %collective-permute-start.7 = (f32[16,1024]{1,0:T(8,128)S(1)}, f32[16,1024]{1,0:T(8,128)S(1)}, u32[]{:S(2)}, u32[]{:S(2)}) collective-permute-start(f32[16,1024]{1,0:T(8,128)S(1)} %get-tuple-element.44), channel_id=1, source_target_pairs={{1,0},{2,1},{3,2},{5,4},{6,5},{7,6},{9,8},{10,9},{11,10},{13,12},{... | collective-permute-start | bytes 196616 | tf_op jit(solution)/shard_map/ppermute | solution.py:25
  162.4 8.3 %collective-permute-start.10 = (f32[16,1024]{1,0:T(8,128)S(1)}, f32[16,1024]{1,0:T(8,128)S(1)}, u32[]{:S(2)}, u32[]{:S(2)}) collective-permute-start(f32[16,1024]{1,0:T(8,128)S(1)} %slice_add_fusion.12), channel_id=1, source_target_pairs={{0,1},{1,2},{2,3},{4,5},{5,6},{6,7},{8,9},{9,10},{10,11},{12,13},{... | collective-permute-start | bytes 196616 | tf_op jit(solution)/shard_map/ppermute | solution.py:29
  170.8 11.9 %collective-permute-start.13 = (f32[16,1024]{1,0:T(8,128)S(1)}, f32[16,1024]{1,0:T(8,128)S(1)}, u32[]{:S(2)}, u32[]{:S(2)}) collective-permute-start(f32[16,1024]{1,0:T(8,128)S(1)} %get-tuple-element.41), channel_id=1, source_target_pairs={{1,0},{2,1},{3,2},{5,4},{6,5},{7,6},{9,8},{10,9},{11,10},{13,12},{... | collective-permute-start | bytes 196616 | tf_op jit(solution)/shard_map/ppermute | solution.py:25
  172.9 5.8 %collective-permute-start.11 = (f32[2,16]{1,0:T(2,128)S(1)}, f32[2,16]{1,0:T(2,128)S(1)}, u32[]{:S(2)}, u32[]{:S(2)}) collective-permute-start(f32[2,16]{1,0:T(2,128)S(1)} %pad_maximum_fusion.14), channel_id=1, source_target_pairs={{0,1},{1,0},{2,3},{3,2},{4,5},{5,4},{6,7},{7,6},{8,9},{9,8},{10,11... | collective-permute-start | bytes 392 | tf_op jit(solution)/shard_map/ppermute | solution.py:21
  173.5 10.0 %collective-permute-start.14 = (f32[16,1024]{1,0:T(8,128)S(1)}, f32[16,1024]{1,0:T(8,128)S(1)}, u32[]{:S(2)}, u32[]{:S(2)}) collective-permute-start(f32[16,1024]{1,0:T(8,128)S(1)} %slice_add_fusion.6), channel_id=1, source_target_pairs={{0,1},{1,2},{2,3},{4,5},{5,6},{6,7},{8,9},{9,10},{10,11},{12,13},{... | collective-permute-start | bytes 196616 | tf_op jit(solution)/shard_map/ppermute | solution.py:29
  178.7 4.0 %collective-permute-start.12 = (f32[2,16]{1,0:T(2,128)S(1)}, f32[2,16]{1,0:T(2,128)S(1)}, u32[]{:S(2)}, u32[]{:S(2)}) collective-permute-start(f32[2,16]{1,0:T(2,128)S(1)} %fusion.101), channel_id=1, source_target_pairs={{0,2},{2,0},{1,3},{3,1},{4,6},{6,4},{5,7},{7,5},{8,10},{10,8},{9,1... | collective-permute-start | bytes 392 | tf_op jit(solution)/shard_map/ppermute | solution.py:21
  186.5 8.6 %collective-permute-start.17 = (f32[16,1024]{1,0:T(8,128)S(1)}, f32[16,1024]{1,0:T(8,128)S(1)}, u32[]{:S(2)}, u32[]{:S(2)}) collective-permute-start(f32[16,1024]{1,0:T(8,128)S(1)} %get-tuple-element.35), channel_id=1, source_target_pairs={{1,0},{2,1},{3,2},{5,4},{6,5},{7,6},{9,8},{10,9},{11,10},{13,12},{... | collective-permute-start | bytes 196616 | tf_op jit(solution)/shard_map/ppermute | solution.py:25
  189.7 6.3 %collective-permute-start.18 = (f32[16,1024]{1,0:T(8,128)S(1)}, f32[16,1024]{1,0:T(8,128)S(1)}, u32[]{:S(2)}, u32[]{:S(2)}) collective-permute-start(f32[16,1024]{1,0:T(8,128)S(1)} %slice_add_fusion), channel_id=1, source_target_pairs={{0,1},{1,2},{2,3},{4,5},{5,6},{6,7},{8,9},{9,10},{10,11},{12,13},{... | collective-permute-start | bytes 196616 | tf_op jit(solution)/shard_map/ppermute | solution.py:29
  197.6 4.4 %collective-permute-start.20 = (f32[7,16]{1,0:T(8,128)S(1)}, f32[7,16]{1,0:T(8,128)S(1)}, u32[]{:S(2)}, u32[]{:S(2)}) collective-permute-start(f32[7,16]{1,0:T(8,128)S(1)} %add.467), channel_id=1, source_target_pairs={{0,2},{2,0},{1,3},{3,1},{4,6},{6,4},{5,7},{7,5},{8,10},{10,8},{9,1... | collective-permute-start | bytes 1352 | tf_op jit(solution)/shard_map/ppermute | solution.py:21
  (10 other events, 46.4 us)
Sparse Core Ops, SparseCore 0:
  29.9 40.2 reduce-scatter.1
  113.9 37.7 all-gather.1
